TPU v7x, 128 devices: a whole 4x4x4 slice. The times are simulated.
128 devices in a mesh: expert: 32 (over z, y, x_hi), dp: 4 (over x_lo, core).
Axes of the slice: x: 4 (x_hi: 2, x_lo: 2; x = x_hi * 2 + x_lo), y: 4, z: 4, core: 2. Of those that a mesh axis runs over, the one named last changes fastest.
Arguments:
- tokens: bfloat16 [16384, 3584], P(('expert', 'dp')), may hold values from -6 to 6
- out_grad: bfloat16 [16384, 3584], P(('expert', 'dp')), may hold values from -2 to 2
- expert_ids: int32 [16384, 8], P(('expert', 'dp')), may hold values from 0 to 255, as said below
- route_weights: bfloat16 [16384, 8], P(('expert', 'dp')), may hold values from 0.099609375 to 1
- w_gate: bfloat16 [32, 3584, 1024], P('expert', None, 'dp'), may hold values from -0.09375 to 0.09375
- w_up: bfloat16 [32, 3584, 1024], P('expert', None, 'dp'), may hold values from -0.09375 to 0.09375
- w_down: bfloat16 [32, 1024, 3584], P('expert', 'dp'), may hold values from -0.1875 to 0.1875
Outputs:
- grad_tokens: bfloat16 [16384, 3584], P(('expert', 'dp'))
- grad_route: bfloat16 [16384, 8], P(('expert', 'dp'))
- grad_gate: bfloat16 [32, 3584, 1024], P('expert', None, 'dp')
- grad_upproj: bfloat16 [32, 3584, 1024], P('expert', None, 'dp')
- grad_down: bfloat16 [32, 1024, 3584], P('expert', 'dp')
Inputs may be any that keep to these rules, and one draw needn't show every extreme that they name: `expert_ids`: each token's 8 ids are distinct. Ids below 32 are the window's experts. Within the 128 tokens of one device no id below 32 appears more than 5 times.
All inputs are finite; a program needn't handle non-finite values.
Results may differ from a plain program's by a relative error of at most 0.015.
Values may be sent and summed in bfloat16 or wider, within the bound.
A program may use at most 128 MiB of HBM per device.

v0:
```python
import jax
import jax.numpy as jnp
from jax import lax
from jax.sharding import PartitionSpec as P


def build_slots(expert_ids, expert_count, capacity):
    flat_ids = expert_ids.reshape(-1)
    onehot = (flat_ids[:, None] == jnp.arange(expert_count, dtype=jnp.int32)[None, :]).astype(
        jnp.int32
    )
    ranking = jnp.sum((jnp.cumsum(onehot, axis=0) - 1) * onehot, axis=1)
    target = jnp.where(
        flat_ids < expert_count, flat_ids * capacity + ranking, expert_count * capacity
    )
    source = jnp.arange(flat_ids.shape[0], dtype=jnp.int32)
    return jnp.full((expert_count * capacity,), -1, jnp.int32).at[target].set(source, mode="drop")


def repeat_groups(values, group_count):
    lead = values.shape[0]
    widened = jnp.broadcast_to(values[:, None], (lead, group_count) + values.shape[1:])
    return widened.reshape((lead * group_count,) + values.shape[1:])


def backward_rows(x_rows, dy_rows, weight_rows, gate_w, up_w, down_w):
    gate_value = jnp.dot(x_rows, gate_w, preferred_element_type=jnp.float32)
    up_value = jnp.dot(x_rows, up_w, preferred_element_type=jnp.float32)
    sigmoid_gate = jax.nn.sigmoid(gate_value)
    hidden = (gate_value * sigmoid_gate * up_value).astype(jnp.bfloat16)
    back_proj = lax.dot_general(
        dy_rows, down_w, (((1,), (1,)), ((), ())), preferred_element_type=jnp.float32
    )
    hidden_f = hidden.astype(jnp.float32)
    route_part = jnp.sum(hidden_f * back_proj, axis=1)
    weight = weight_rows.astype(jnp.float32)[:, None]
    scaled = weight * back_proj
    d_gate = (scaled * up_value * sigmoid_gate * (1.0 + gate_value * (1.0 - sigmoid_gate))).astype(
        jnp.bfloat16
    )
    d_up = (scaled * gate_value * sigmoid_gate).astype(jnp.bfloat16)
    weighted = (weight * hidden_f).astype(jnp.bfloat16)
    contract_rows = (((0,), (0,)), ((), ()))
    grad_g = lax.dot_general(
        x_rows, d_gate, contract_rows, preferred_element_type=jnp.float32
    ).astype(jnp.bfloat16)
    grad_u = lax.dot_general(
        x_rows, d_up, contract_rows, preferred_element_type=jnp.float32
    ).astype(jnp.bfloat16)
    grad_d = lax.dot_general(
        weighted, dy_rows, contract_rows, preferred_element_type=jnp.float32
    ).astype(jnp.bfloat16)
    contract_hidden = (((1,), (1,)), ((), ()))
    partial_value = lax.dot_general(
        d_gate, gate_w, contract_hidden, preferred_element_type=jnp.float32
    )
    partial_value = partial_value + lax.dot_general(
        d_up, up_w, contract_hidden, preferred_element_type=jnp.float32
    )
    return (partial_value, route_part, grad_g, grad_u, grad_d)


def shards(tokens, out_grad, expert_ids, route_weights, w_gate, w_up, w_down):
    expert_count = lax.axis_size("expert")
    group_count = lax.axis_size("dp")
    token_rows, width = tokens.shape
    route_count = expert_ids.shape[1]
    capacity = 5 * token_rows // (4 * expert_count)
    slot_table = build_slots(expert_ids, expert_count, capacity)
    occupied = slot_table >= 0
    clamped = jnp.where(occupied, slot_table, 0)
    owner_token = clamped // route_count
    zero_row = jnp.zeros((), jnp.bfloat16)
    x_send = jnp.where(occupied[:, None], tokens[owner_token], zero_row).reshape(
        expert_count, capacity, width
    )
    dy_send = jnp.where(occupied[:, None], out_grad[owner_token], zero_row).reshape(
        expert_count, capacity, width
    )
    w_send = jnp.where(occupied, route_weights.reshape(-1)[clamped], zero_row).reshape(
        expert_count, capacity
    )
    x_all, dy_all, w_all = (
        lax.all_to_all(
            repeat_groups(x_send, group_count),
            ("expert", "dp"),
            split_axis=0,
            concat_axis=0,
            tiled=True,
        ),
        lax.all_to_all(
            repeat_groups(dy_send, group_count),
            ("expert", "dp"),
            split_axis=0,
            concat_axis=0,
            tiled=True,
        ),
        lax.all_to_all(
            repeat_groups(w_send, group_count),
            ("expert", "dp"),
            split_axis=0,
            concat_axis=0,
            tiled=True,
        ),
    )
    partial_value, route_part, grad_g, grad_u, grad_d = backward_rows(
        x_all.reshape(-1, width),
        dy_all.reshape(-1, width),
        w_all.reshape(-1),
        w_gate[0],
        w_up[0],
        w_down[0],
    )
    part_rows = partial_value.astype(jnp.bfloat16).reshape(
        expert_count * group_count, capacity, width
    )
    part_route = route_part.astype(jnp.bfloat16).reshape(expert_count * group_count, capacity)
    got_rows, got_route = (
        lax.all_to_all(part_rows, ("expert", "dp"), split_axis=0, concat_axis=0, tiled=True),
        lax.all_to_all(part_route, ("expert", "dp"), split_axis=0, concat_axis=0, tiled=True),
    )
    return_rows = jnp.sum(
        got_rows.reshape(expert_count, group_count, capacity, width).astype(jnp.float32), axis=1
    ).astype(jnp.bfloat16)
    return_route = jnp.sum(
        got_route.reshape(expert_count, group_count, capacity).astype(jnp.float32), axis=1
    ).astype(jnp.bfloat16)
    picker = (
        (owner_token[None, :] == jnp.arange(token_rows, dtype=jnp.int32)[:, None])
        & occupied[None, :]
    ).astype(jnp.bfloat16)
    grad_tokens = jnp.dot(
        picker, return_rows.reshape(-1, width), preferred_element_type=jnp.float32
    ).astype(jnp.bfloat16)
    route_match = (
        slot_table[None, :] == jnp.arange(token_rows * route_count, dtype=jnp.int32)[:, None]
    )
    route_values = return_route.reshape(-1).astype(jnp.float32)
    grad_route = jnp.sum(jnp.where(route_match, route_values[None, :], 0.0), axis=1)
    grad_route = grad_route.reshape(token_rows, route_count).astype(jnp.bfloat16)
    return (grad_tokens, grad_route, grad_g[None], grad_u[None], grad_d[None])


def solution(mesh):
    in_specs = (
        P(("expert", "dp"), None),
        P(("expert", "dp"), None),
        P(("expert", "dp"), None),
        P(("expert", "dp"), None),
        P("expert", None, "dp"),
        P("expert", None, "dp"),
        P("expert", "dp", None),
    )
    out_specs = (
        P(("expert", "dp"), None),
        P(("expert", "dp"), None),
        P("expert", None, "dp"),
        P("expert", None, "dp"),
        P("expert", "dp", None),
    )
    return jax.shard_map(shards, mesh=mesh, in_specs=in_specs, out_specs=out_specs, check_vma=False)
```

profile of v0, /device:TPU:3, one launch (start us, length us, event | category | flops | bytes accessed | tf_op | source)
XLA Modules:
  0.0 381.8 jit_solution(6323423083841290254)
XLA Ops:
  0.7 0.8 broadcast_compare_fusion
  1.5 0.7 broadcast_multiply_fusion
  2.2 0.8 copy.47
  3.2 0.1 copy.45
  3.3 0.1 lt.36
  3.4 0.8 copy.51
  4.5 9.0 %reduce-window.6 = s32[32,8,128]{2,1,0:T(8,128)S(1)} reduce-window(s32[32,8,128]{2,1,0:T(8,128)S(1)} %fusion.18, s32[]{:T(128)} %constant.18.clone.1), window={size=1x1x128 pad=0_0x0_0x127_0}, to_apply=%region_0.0 | reduce-window | flops 4161536 | bytes 262148 | tf_op jit(solution)/shard_map/reduce-window
  13.6 0.1 copy.49
  14.1 4.3 %scatter_custom_fusion = s32[160]{0:T(256)S(1)} fusion(s32[1024]{0:T(1024)S(1)} %bitcast.64, s32[1024]{0:T(1024)S(1)} %iota.19, s32[]{:T(128)} %constant.14.clone.1), kind=kCustom, calls=%fused_computation.59 | custom fusion | bytes 644 | tf_op jit(solution)/shard_map/scatter | solution.py:17
  18.4 1.6 gather_fusion
  20.3 0.1 all_to_all.19
  20.5 0.8 copy.53
  21.2 10.8 %all-to-all-start = ((bf16[128,1,5]{2,1,0:T(2,128)(2,1)}), bf16[128,1,5]{2,1,0:T(2,128)(2,1)S(1)}, u32[]{:S(2)}, u32[]{:S(2)}) async-start(bf16[128,1,5]{2,1,0:T(2,128)(2,1)} %copy.53), calls=%async_computation | async-start | bytes 131072 | tf_op jit(solution)/shard_map/all_to_all | solution.py:98
  32.1 0.1 broadcast_in_dim.93
  32.2 2.3 gather_fusion.2
  34.5 2.6 gather.17
  37.1 2.3 gather_fusion.1
  39.4 2.5 gather.15
  41.9 4.3 %broadcast_select_fusion.1 = (bf16[32,5,3584]{2,1,0:T(8,128)(2,1)}, bf16[32,5,3584]{2,1,0:T(8,128)(2,1)}) fusion(bf16[32,5,3584]{2,1,0:T(8,128)(2,1)} %gather.15, pred[32,5]{1,0:T(8,128)(4,1)S(1)} %broadcast_in_dim.93, bf16[32,5,3584]{2,1,0:T(8,128)(2,1)} %gather.17), kind=kLoop, calls=%fused_computation.23 | loop fusion | flops 1146880 | bytes 4587680 | tf_op jit(solution)/shard_map/jit(_where)/select_n | solution.py:77
  46.2 2.0 broadcast_in_dim.98
  48.3 95.1 %all_to_all.30 = bf16[128,5,3584]{2,1,0:T(8,128)(2,1)} all-to-all(bf16[128,5,3584]{2,1,0:T(8,128)(2,1)S(1)} %bitcast.58), channel_id=1, replica_groups=mesh['expert'=32,'dp'=4] {'expert','dp'}, dimensions={0} | all-to-all | bytes 9175040 | tf_op jit(solution)/shard_map/all_to_all | solution.py:84
  143.4 3.5 broadcast_in_dim.97
  146.9 6.7 %all-to-all-start.1 = ((bf16[128,5,3584]{2,1,0:T(8,128)(2,1)}), bf16[128,5,3584]{2,1,0:T(8,128)(2,1)}, u32[]{:S(2)}, u32[]{:S(2)}) async-start(bf16[128,5,3584]{2,1,0:T(8,128)(2,1)} %bitcast.57), calls=%async_computation.1 | async-start | bytes 14680064 | tf_op jit(solution)/shard_map/all_to_all | solution.py:91
  153.7 0.2 convert_reduce_fusion
  153.8 0.2 reshape.176
  154.1 8.1 %reshape.171 = bf16[640,3584]{1,0:T(8,128)(2,1)} reshape(bf16[128,5,3584]{2,1,0:T(8,128)(2,1)} %all_to_all.30) | data formatting | bytes 9175040 | tf_op jit(solution)/shard_map/reshape | solution.py:107
  162.1 4.9 %fusion.5 = f32[640,256]{0,1:T(8,128)} fusion(bf16[640,3584]{1,0:T(8,128)(2,1)} %reshape.171, bf16[1,3584,256]{2,1,0:T(8,128)(2,1)S(1)} %copy-done), kind=kOutput, calls=%fused_computation.15 | convolution fusion | flops 1174405120 | bytes 7077888 | tf_op jit(solution)/shard_map/dot_general | solution.py:27
  167.1 2.6 fusion.8
  169.6 71.5 %all-to-all-done.1 = bf16[128,5,3584]{2,1,0:T(8,128)(2,1)} async-done(((bf16[128,5,3584]{2,1,0:T(8,128)(2,1)}), bf16[128,5,3584]{2,1,0:T(8,128)(2,1)}, u32[]{:S(2)}, u32[]{:S(2)}) %all-to-all-start.1) | async-done | bytes 4587552 | tf_op jit(solution)/shard_map/all_to_all | solution.py:91
  241.1 8.1 %reshape.169 = bf16[640,3584]{1,0:T(8,128)(2,1)} reshape(bf16[128,5,3584]{2,1,0:T(8,128)(2,1)} %all-to-all-done.1) | data formatting | bytes 9175040 | tf_op jit(solution)/shard_map/reshape | solution.py:108
  249.2 4.9 %fusion.12 = (bf16[640]{0:T(1024)(128)(2,1)S(1)}, bf16[640,256]{0,1:T(8,128)(2,1)S(1)}, bf16[640,256]{0,1:T(8,128)(2,1)S(1)}, bf16[640,256]{0,1:T(8,128)(2,1)S(1)}) fusion(f32[640,256]{0,1:T(8,128)} %fusion.8, f32[640,256]{0,1:T(8,128)} %fusion.5, f32[640]{0:T(1024)S(1)} %reshape.176, bf16[640,3584]{1,0:T(8,128)(2,1)} %reshape.169, ...), kind=kOutput, calls=%fused_computation.26 | convolution fusion | flops 1177681280 | bytes 8720128 | tf_op jit(solution)/shard_map/dot_general | solution.py:31
  254.1 0.9 convert_element_type.101
  255.0 6.9 %all-to-all-start.4 = ((bf16[128,1,5]{2,1,0:T(2,128)(2,1)}), bf16[128,1,5]{2,1,0:T(2,128)(2,1)S(1)}, u32[]{:S(2)}, u32[]{:S(2)}) async-start(bf16[128,1,5]{2,1,0:T(2,128)(2,1)} %convert_element_type.101), calls=%async_computation.4 | async-start | bytes 131072 | tf_op jit(solution)/shard_map/all_to_all | solution.py:120
  261.9 1.4 fusion.3
  263.4 3.5 add_convert_fusion
  266.9 7.8 %reshape.172 = bf16[128,5,3584]{2,1,0:T(8,128)(2,1)} reshape(bf16[640,3584]{1,0:T(8,128)(2,1)} %add_convert_fusion) | data formatting | bytes 9175040 | tf_op jit(solution)/shard_map/reshape | solution.py:114
  274.8 10.2 %all-to-all-start.3 = ((bf16[128,5,3584]{2,1,0:T(8,128)(2,1)}), bf16[128,5,3584]{2,1,0:T(8,128)(2,1)}, u32[]{:S(2)}, u32[]{:S(2)}) async-start(bf16[128,5,3584]{2,1,0:T(8,128)(2,1)} %reshape.172), calls=%async_computation.3 | async-start | bytes 14680064 | tf_op jit(solution)/shard_map/all_to_all | solution.py:119
  284.9 5.3 %fusion = bf16[1,3584,256]{2,1,0:T(8,128)(2,1)} fusion(bf16[640,3584]{1,0:T(8,128)(2,1)} %reshape.171, bf16[640,256]{0,1:T(8,128)(2,1)S(1)} %get-tuple-element.29), kind=kOutput, calls=%fused_computation.9 | convolution fusion | flops 1175322624 | bytes 6750208 | tf_op jit(solution)/shard_map/dot_general | solution.py:44
  290.3 5.2 %fusion.1 = bf16[1,3584,256]{2,1,0:T(8,128)(2,1)} fusion(bf16[640,3584]{1,0:T(8,128)(2,1)} %reshape.171, bf16[640,256]{0,1:T(8,128)(2,1)S(1)} %get-tuple-element.30), kind=kOutput, calls=%fused_computation.10 | convolution fusion | flops 1175322624 | bytes 6750208 | tf_op jit(solution)/shard_map/dot_general | solution.py:47
  295.5 2.8 fusion.2
  298.4 0.1 reshape.175
  298.8 0.1 reshape.177
  298.9 0.1 select_reduce_fusion
  299.1 0.7 copy.57
  299.8 72.5 %all-to-all-done.3 = bf16[128,5,3584]{2,1,0:T(8,128)(2,1)} async-done(((bf16[128,5,3584]{2,1,0:T(8,128)(2,1)}), bf16[128,5,3584]{2,1,0:T(8,128)(2,1)}, u32[]{:S(2)}, u32[]{:S(2)}) %all-to-all-start.3) | async-done | bytes 4587552 | tf_op jit(solution)/shard_map/all_to_all | solution.py:119
  372.3 6.5 %bitcast_reduce_fusion = bf16[32,5,3584]{2,1,0:T(8,128)(2,1)} fusion(bf16[128,5,3584]{2,1,0:T(8,128)(2,1)} %all-to-all-done.3), kind=kLoop, calls=%fused_computation.5 | loop fusion | flops 1720320 | bytes 5734400 | tf_op jit(solution)/shard_map/reduce_sum | solution.py:122
  378.8 1.7 reshape.174
  380.5 1.3 convolution_convert_fusion.3
  (46 shorter events, 1.7 us)
Async XLA Ops:
  0.6 161.5 %copy-start = (bf16[1,3584,256]{2,1,0:T(8,128)(2,1)S(1)}, bf16[1,3584,256]{2,1,0:T(8,128)(2,1)}, u32[]{:S(2)}) copy-start(bf16[1,3584,256]{2,1,0:T(8,128)(2,1)} %param.11) | copy-start | bytes 5505028
  0.6 31.6 %copy-start.1 = (bf16[128,3584]{1,0:T(8,128)(2,1)S(1)}, bf16[128,3584]{1,0:T(8,128)(2,1)}, u32[]{:S(2)}) copy-start(bf16[128,3584]{1,0:T(8,128)(2,1)} %param.7) | copy-start | bytes 2752516
  21.2 24.9 %all-to-all-start = ((bf16[128,1,5]{2,1,0:T(2,128)(2,1)}), bf16[128,1,5]{2,1,0:T(2,128)(2,1)S(1)}, u32[]{:S(2)}, u32[]{:S(2)}) async-start(bf16[128,1,5]{2,1,0:T(2,128)(2,1)} %copy.53), calls=%async_computation | async-start | bytes 131072 | tf_op jit(solution)/shard_map/all_to_all | solution.py:98
  34.5 2.6 copy-start.2
  48.2 95.2 %copy-start.3 = (bf16[32,5,3584]{2,1,0:T(8,128)(2,1)S(1)}, bf16[32,5,3584]{2,1,0:T(8,128)(2,1)}, u32[]{:S(2)}) copy-start(bf16[32,5,3584]{2,1,0:T(8,128)(2,1)} %get-tuple-element.31) | copy-start | bytes 3440644
  146.9 94.2 %all-to-all-start.1 = ((bf16[128,5,3584]{2,1,0:T(8,128)(2,1)}), bf16[128,5,3584]{2,1,0:T(8,128)(2,1)}, u32[]{:S(2)}, u32[]{:S(2)}) async-start(bf16[128,5,3584]{2,1,0:T(8,128)(2,1)} %bitcast.57), calls=%async_computation.1 | async-start | bytes 14680064 | tf_op jit(solution)/shard_map/all_to_all | solution.py:91
  162.1 4.9 %copy-start.4 = (bf16[640,3584]{1,0:T(8,128)(2,1)S(1)}, bf16[640,3584]{1,0:T(8,128)(2,1)}, u32[]{:S(2)}) copy-start(bf16[640,3584]{1,0:T(8,128)(2,1)} %reshape.171) | copy-start | bytes 13762564
  162.1 4.9 %copy-start.5 = (bf16[1,3584,256]{2,1,0:T(8,128)(2,1)S(1)}, bf16[1,3584,256]{2,1,0:T(8,128)(2,1)}, u32[]{:S(2)}) copy-start(bf16[1,3584,256]{2,1,0:T(8,128)(2,1)} %param.12) | copy-start | bytes 5505028
  255.0 19.8 %all-to-all-start.4 = ((bf16[128,1,5]{2,1,0:T(2,128)(2,1)}), bf16[128,1,5]{2,1,0:T(2,128)(2,1)S(1)}, u32[]{:S(2)}, u32[]{:S(2)}) async-start(bf16[128,1,5]{2,1,0:T(2,128)(2,1)} %convert_element_type.101), calls=%async_computation.4 | async-start | bytes 131072 | tf_op jit(solution)/shard_map/all_to_all | solution.py:120
  261.9 1.5 copy-start.6
  274.8 97.5 %all-to-all-start.3 = ((bf16[128,5,3584]{2,1,0:T(8,128)(2,1)}), bf16[128,5,3584]{2,1,0:T(8,128)(2,1)}, u32[]{:S(2)}, u32[]{:S(2)}) async-start(bf16[128,5,3584]{2,1,0:T(8,128)(2,1)} %reshape.172), calls=%async_computation.3 | async-start | bytes 14680064 | tf_op jit(solution)/shard_map/all_to_all | solution.py:119
  284.9 10.6 %slice-start = ((s8[4587520]{0:T(1024)(128)(4,1)}), s8[4194304]{0:T(1024)(128)(4,1)S(1)}, s32[]{:S(2)}) async-start(s8[4587520]{0:T(1024)(128)(4,1)} %bitcast.59), calls=%async_computation.5 | async-start | bytes 8388608
  290.3 5.2 %slice-start.1 = ((s8[4587520]{0:T(1024)(128)(4,1)}), s8[393216]{0:T(1024)(128)(4,1)S(1)}, s32[]{:S(2)}) async-start(s8[4587520]{0:T(1024)(128)(4,1)} %bitcast.59), calls=%async_computation.6 | async-start | bytes 786432
where the time goes:
time: 383 us; the launch traced here: 382 us
  waiting for transfers between devices  144 us (38%)
  blocking collectives  95.1 us (25%)
  local copies, waits for them, and re-layouts  53.1 us (14%)
  starting transfers between devices  34.7 us (9%)
  matrix products  32 us (8%)
  other arithmetic  22 us (6%)
    all_to_all x1, blocking collectives, shards(): lax.all_to_all(repeat_groups(x_send, group_count), ('expert', 'dp'), spli...  95.1 us
    all_to_all x1, waiting for transfers between devices, shards(): lax.all_to_all(part_rows, ('expert', 'dp'), split_axis=0, concat_axis=0,...  72.5 us
    all_to_all x1, waiting for transfers between devices, shards(): lax.all_to_all(repeat_groups(dy_send, group_count), ('expert', 'dp'), spl...  71.5 us
    all_to_all x1, starting transfers between devices, shards(): lax.all_to_all(repeat_groups(w_send, group_count), ('expert', 'dp'), spli...  10.8 us
    all_to_all x1, starting transfers between devices, shards(): lax.all_to_all(part_rows, ('expert', 'dp'), split_axis=0, concat_axis=0,...  10.2 us
    another operation x2, other arithmetic  9.04 us
    reshape x1, local copies, waits for them, and re-layouts, shards(): x_all.reshape(-1, width)  8.09 us
    reshape x1, local copies, waits for them, and re-layouts, shards(): dy_all.reshape(-1, width)  8.06 us
  transfers between devices with their start and end apart: 4, of which 2 were waited for; matrix products, arithmetic and copies ran while one was open for 15% of the time, Pallas kernels for 0%

commit v1 on v0

v1 whole, which is shorter than its diff:
```python
import jax
import jax.numpy as jnp
from jax import lax
from jax.experimental import pallas as pl
from jax.experimental.pallas import tpu as pltpu
from jax.sharding import PartitionSpec as P

NZ, NY, NX = 4, 4, 2
EXP = NZ * NY * NX
CAP = 5
STEP = 4
CHUNKS = EXP // STEP
LANES = 128
FEAT = 3584
HID = 256
COLS = FEAT // LANES
FROWS = 288
RROWS = 144
SRC = 4 * STEP
ROWS = SRC * CAP
ALL = ROWS * CHUNKS
TOK = 128
MESH = pl.DeviceIdType.MESH
F32, BF16 = jnp.float32, jnp.bfloat16


def shifted(e, k, sign):
    z, y, x = e // (NY * NX), (e // NX) % NY, e % NX
    kz, ky, kx = k // (NY * NX), (k // NX) % NY, k % NX
    z = (z + NZ + sign * kz) % NZ
    y = (y + NY + sign * ky) % NY
    x = (x + NX + sign * kx) % NX
    return (z * NY + y) * NX + x


def body(
    ids_ref, rw_ref, tok_ref, dy_ref, wg_hbm, wu_hbm, wd_hbm,
    gt_ref, gr_ref, gg_hbm, gu_hbm, gd_hbm,
    wg, wu, wd, flat, send, recv, rows, dgu, wtd, retf, own, pst, prt, rsend, ret, slots, got, sg, su, sd,
    send_sem, recv_sem, fws_sem, fwr_sem, pas_sem, par_sem, rs_sem, ret_sem, win_sem, out_sem,
):
    e = lax.axis_index("expert")
    d = lax.axis_index("dp")
    xl, c = d // 2, d % 2
    partner = {"expert": e, "dp": xl * 2 + 1 - c}

    loads = [
        pltpu.make_async_copy(h, v, win_sem.at[i])
        for i, (h, v) in enumerate(((wg_hbm, wg), (wu_hbm, wu), (wd_hbm, wd)))
    ]
    for copy in loads:
        copy.start()

    kk = lax.broadcasted_iota(jnp.int32, (EXP, TOK), 0)
    z, y, x = e // (NY * NX), (e // NX) % NY, e % NX
    tz = (z + (kk >> 3)) & 3
    ty = (y + ((kk >> 1) & 3)) & 3
    tx = (x + (kk & 1)) & 1
    target = tz * (NY * NX) + ty * NX + tx
    chosen = jnp.zeros((EXP, TOK), F32)
    weight = jnp.zeros((EXP, TOK), F32)
    for q in range(8):
        same = ids_ref[q : q + 1, :] == target
        chosen = chosen + jnp.where(same, 1.0, 0.0)
        weight = weight + jnp.where(same, rw_ref[q : q + 1, :], 0.0)
    before = lax.broadcasted_iota(jnp.int32, (TOK, TOK), 0) < lax.broadcasted_iota(
        jnp.int32, (TOK, TOK), 1
    )
    rank = jnp.dot(
        chosen.astype(BF16), jnp.where(before, 1.0, 0.0).astype(BF16), preferred_element_type=F32
    )
    for j in range(CAP):
        hot = jnp.where(jnp.abs(rank - j) < 0.5, chosen, 0.0)
        slots[j * EXP : (j + 1) * EXP, :] = hot.astype(BF16)
        one = jnp.sum(hot * weight, axis=1, keepdims=True)
        flat[pl.ds(2 * CAP * COLS + j, EXP, stride=FROWS), :] = jnp.broadcast_to(one, (EXP, LANES))
    for j in range(2 * CAP * COLS + CAP, FROWS):
        flat[pl.ds(j, EXP, stride=FROWS), :] = jnp.zeros((EXP, LANES), F32)
    for j in range(CAP * COLS + 1, RROWS):
        retf[pl.ds(j, SRC, stride=RROWS), :] = jnp.zeros((SRC, LANES), F32)

    def gather(m, carry):
        for a, ref in enumerate((tok_ref, dy_ref)):
            picked = jnp.dot(
                slots[...], ref[:, pl.ds(pl.multiple_of(m * 256, 256), 256)], preferred_element_type=F32
            )
            for h in range(2):
                for j in range(CAP):
                    at = j * 2 * COLS + a * COLS + m * 2 + h
                    flat[pl.ds(at, EXP, stride=FROWS), :] = picked[
                        j * EXP : (j + 1) * EXP, h * LANES : (h + 1) * LANES
                    ]
        return carry

    lax.fori_loop(0, FEAT // 256, gather, 0)

    def remote(k, xd):
        g, kq = k // STEP, k % STEP
        return pltpu.make_async_remote_copy(
            src_ref=send.at[k],
            dst_ref=recv.at[g, c * (2 * STEP) + kq * 2 + xl],
            send_sem=send_sem.at[k * 2 + xd],
            recv_sem=recv_sem.at[g],
            device_id={"expert": shifted(e, k, 1), "dp": xd * 2 + c},
            device_id_type=MESH,
        )

    send[0] = flat[0:FROWS, :].astype(BF16)
    remote(0, 1 - xl).start()
    pltpu.make_async_copy(send.at[0], recv.at[0, c * (2 * STEP) + xl], recv_sem.at[0]).start()

    def issue(k, carry):
        send[k] = flat[pl.ds(pl.multiple_of(k * FROWS, 8), FROWS), :].astype(BF16)
        remote(k, 0).start()
        remote(k, 1).start()
        return carry

    lax.fori_loop(1, EXP, issue, 0)
    for copy in loads:
        copy.wait()

    def half(g, core):
        return recv.at[g, pl.ds(core * (2 * STEP), 2 * STEP)]

    def forward(g):
        return pltpu.make_async_remote_copy(
            src_ref=half(g, c), dst_ref=half(g, c), send_sem=fws_sem.at[g], recv_sem=fwr_sem.at[g],
            device_id=partner, device_id_type=MESH,
        )

    def take(g):
        pltpu.make_async_copy(half(g, c), half(g, c), recv_sem.at[g]).wait()
        forward(g).start()

    def part(g):
        return pltpu.make_async_remote_copy(
            src_ref=pst.at[g], dst_ref=prt.at[g], send_sem=pas_sem.at[g], recv_sem=par_sem.at[g],
            device_id=partner, device_id_type=MESH,
        )

    def back(g, i, xs):
        kq = i // 2
        return pltpu.make_async_remote_copy(
            src_ref=rsend.at[g, pl.ds(pl.multiple_of((kq * 2 + xs) * RROWS, 16), RROWS)],
            dst_ref=ret.at[g, xl * STEP + kq],
            send_sem=rs_sem.at[g * (2 * STEP) + i],
            recv_sem=ret_sem.at[g],
            device_id={"expert": shifted(e, g * STEP + kq, -1), "dp": xs * 2 + c},
            device_id_type=MESH,
        )

    def compute(g):
        def widen(s, carry):
            flat[pl.ds(pl.multiple_of(s * FROWS, 8), FROWS), :] = recv[g, s].astype(F32)
            return carry

        lax.fori_loop(0, SRC, widen, 0)
        base = pl.multiple_of(g * ROWS, 16)

        def order(q, carry):
            for h in range(4):
                col = q * 4 + h
                for j in range(CAP):
                    piece = flat[pl.ds(j * 2 * COLS + col, SRC, stride=FROWS), :]
                    rows[
                        pl.ds(pl.multiple_of(base + j * SRC, 16), SRC),
                        pl.ds(pl.multiple_of(col * LANES, LANES), LANES),
                    ] = piece.astype(BF16)
            return carry

        lax.fori_loop(0, 2 * COLS // 4, order, 0)
        weights = jnp.concatenate(
            [flat[pl.ds(2 * CAP * COLS + j, SRC, stride=FROWS), :] for j in range(CAP)], axis=0
        )
        weights = jnp.concatenate([weights, weights], axis=1)
        xs = rows[pl.ds(base, ROWS), 0:FEAT]
        dys = rows[pl.ds(base, ROWS), FEAT : 2 * FEAT]
        gate = jnp.dot(xs, wg[...], preferred_element_type=F32)
        up = jnp.dot(xs, wu[...], preferred_element_type=F32)
        proj = lax.dot_general(dys, wd[...], (((1,), (1,)), ((), ())), preferred_element_type=F32)
        sig = jax.nn.sigmoid(gate)
        hidden = (gate * sig * up).astype(BF16).astype(F32)
        route = jnp.sum(hidden * proj, axis=1, keepdims=True)
        scaled = weights * proj
        d_gate = (scaled * up * sig * (1.0 + gate * (1.0 - sig))).astype(BF16)
        d_up = (scaled * gate * sig).astype(BF16)
        dgu[pl.ds(base, ROWS), 0:HID] = d_gate
        dgu[pl.ds(base, ROWS), HID : 2 * HID] = d_up
        wtd[pl.ds(base, ROWS), :] = (weights * hidden).astype(BF16)
        lane = lax.broadcasted_iota(jnp.int32, (SRC, LANES), 1)
        line = jnp.zeros((SRC, LANES), F32)
        for j in range(CAP):
            line = line + jnp.where(lane == j, route[j * SRC : (j + 1) * SRC, :], 0.0)
        retf[pl.ds(CAP * COLS, SRC, stride=RROWS), :] = line

        def spread(m, carry):
            cols = pl.ds(pl.multiple_of(m * 256, 256), 256)
            nt = (((1,), (1,)), ((), ()))
            dg = dgu[pl.ds(base, ROWS), 0:HID]
            du = dgu[pl.ds(base, ROWS), HID : 2 * HID]
            piece = lax.dot_general(dg, wg[cols, :], nt, preferred_element_type=F32)
            piece = piece + lax.dot_general(du, wu[cols, :], nt, preferred_element_type=F32)
            for h in range(2):
                for j in range(CAP):
                    retf[pl.ds(j * COLS + m * 2 + h, SRC, stride=RROWS), :] = piece[
                        j * SRC : (j + 1) * SRC, h * LANES : (h + 1) * LANES
                    ]
            return carry

        lax.fori_loop(0, FEAT // 256, spread, 0)
        size = 2 * STEP * RROWS
        pst[g] = retf[pl.ds(pl.multiple_of((1 - c) * size, 8), size), :].astype(BF16)
        part(g).start()
        own[g] = retf[pl.ds(pl.multiple_of(c * size, 8), size), :].astype(BF16)

    def reply(g):
        part(g).wait_recv()
        rsend[g] = (own[g].astype(F32) + prt[g].astype(F32)).astype(BF16)

    def local(g):
        return pltpu.make_async_copy(
            rsend.at[0, pl.ds(pl.multiple_of(xl * RROWS, 16), RROWS)], ret.at[0, xl * STEP], ret_sem.at[0]
        )

    take(0)

    def chunk(g, carry):
        @pl.when(g < CHUNKS - 1)
        def _():
            take(g + 1)

        forward(g).wait_recv()
        compute(g)

        @pl.when(g == 1)
        def _():
            reply(0)
            local(0).start()
            back(0, 0, 1 - xl).start()
            for i in range(2, 2 * STEP):
                back(0, i, i % 2).start()

        @pl.when(g > 1)
        def _():
            reply(g - 1)
            for i in range(2 * STEP):
                back(g - 1, i, i % 2).start()

        return carry

    lax.fori_loop(0, CHUNKS, chunk, 0)
    reply(CHUNKS - 1)
    for i in range(2 * STEP):
        back(CHUNKS - 1, i, i % 2).start()

    tn = (((0,), (0,)), ((), ()))

    def grads(m, carry):
        at = pl.ds(pl.multiple_of(m * 256, 256), 256)
        far = pl.ds(pl.multiple_of(FEAT + m * 256, 256), 256)
        both = lax.dot_general(rows[:, at], dgu[...], tn, preferred_element_type=F32)
        sg[at, :] = both[:, 0:HID].astype(BF16)
        su[at, :] = both[:, HID : 2 * HID].astype(BF16)
        down = lax.dot_general(wtd[...], rows[:, far], tn, preferred_element_type=F32)
        sd[:, at] = down.astype(BF16)
        return carry

    lax.fori_loop(0, FEAT // 256, grads, 0)
    stores = [
        pltpu.make_async_copy(v, h, out_sem.at[i])
        for i, (h, v) in enumerate(((gg_hbm, sg), (gu_hbm, su), (gd_hbm, sd)))
    ]
    for copy in stores:
        copy.start()

    def collect(g, carry):
        pltpu.make_async_copy(ret.at[g], ret.at[g], ret_sem.at[g]).wait()
        for xs in range(2):
            for kq in range(STEP):
                at = (xs * EXP + g * STEP + kq) * RROWS
                flat[pl.ds(pl.multiple_of(at, 8), RROWS), :] = ret[g, xs * STEP + kq].astype(F32)
        return carry

    lax.fori_loop(0, CHUNKS, collect, 0)

    def merge(q, carry):
        for h in range(2):
            col = q * 2 + h
            for j in range(CAP):
                near = flat[pl.ds(j * COLS + col, EXP, stride=RROWS), :]
                far = flat[pl.ds(EXP * RROWS + j * COLS + col, EXP, stride=RROWS), :]
                got[j * EXP : (j + 1) * EXP, pl.ds(pl.multiple_of(col * LANES, LANES), LANES)] = (
                    near + far
                ).astype(BF16)
        return carry

    lax.fori_loop(0, COLS // 2, merge, 0)
    line = (
        flat[pl.ds(CAP * COLS, EXP, stride=RROWS), :]
        + flat[pl.ds(EXP * RROWS + CAP * COLS, EXP, stride=RROWS), :]
    )
    spot = jnp.zeros((EXP, TOK), F32)
    for j in range(CAP):
        spot = spot + slots[j * EXP : (j + 1) * EXP, :].astype(F32) * line[:, j : j + 1]
    for q in range(8):
        gr_ref[q : q + 1, :] = jnp.sum(
            jnp.where(ids_ref[q : q + 1, :] == target, spot, 0.0), axis=0, keepdims=True
        )

    def place(m, carry):
        at = pl.ds(pl.multiple_of(m * 512, 512), 512)
        gt_ref[:, at] = lax.dot_general(slots[...], got[:, at], tn, preferred_element_type=F32).astype(BF16)
        return carry

    lax.fori_loop(0, FEAT // 512, place, 0)

    for copy in stores:
        copy.wait()
    remote(0, 1 - xl).wait_send()
    back(0, 0, 1 - xl).wait_send()

    def drain(k, carry):
        remote(k, 0).wait_send()
        remote(k, 1).wait_send()
        return carry

    lax.fori_loop(1, EXP, drain, 0)

    def drain_back(i, carry):
        pltpu.make_async_copy(
            rsend.at[0, pl.ds(0, RROWS)], rsend.at[0, pl.ds(0, RROWS)], rs_sem.at[i]
        ).wait()
        return carry

    lax.fori_loop(2, CHUNKS * 2 * STEP, drain_back, 0)

    def drain_pairs(g, carry):
        forward(g).wait_send()
        part(g).wait_send()
        return carry

    lax.fori_loop(0, CHUNKS, drain_pairs, 0)


def shards(tokens, out_grad, expert_ids, route_weights, w_gate, w_up, w_down):
    vmem = pl.BlockSpec(memory_space=pltpu.VMEM)
    anywhere = pl.BlockSpec(memory_space=pl.ANY)
    size = 2 * STEP * RROWS
    dma = pltpu.SemaphoreType.DMA
    grad_tokens, grad_route, grad_g, grad_u, grad_d = pl.pallas_call(
        body,
        out_shape=(
            jax.ShapeDtypeStruct((TOK, FEAT), BF16),
            jax.ShapeDtypeStruct((8, TOK), F32),
            jax.ShapeDtypeStruct((FEAT, HID), BF16),
            jax.ShapeDtypeStruct((FEAT, HID), BF16),
            jax.ShapeDtypeStruct((HID, FEAT), BF16),
        ),
        in_specs=[vmem, vmem, vmem, vmem, anywhere, anywhere, anywhere],
        out_specs=(vmem, vmem, anywhere, anywhere, anywhere),
        scratch_shapes=[
            pltpu.VMEM((FEAT, HID), BF16),
            pltpu.VMEM((FEAT, HID), BF16),
            pltpu.VMEM((HID, FEAT), BF16),
            pltpu.VMEM((EXP * FROWS, LANES), F32),
            pltpu.VMEM((EXP, FROWS, LANES), BF16),
            pltpu.VMEM((CHUNKS, SRC, FROWS, LANES), BF16),
            pltpu.VMEM((ALL, 2 * FEAT), BF16),
            pltpu.VMEM((ALL, 2 * HID), BF16),
            pltpu.VMEM((ALL, HID), BF16),
            pltpu.VMEM((SRC * RROWS, LANES), F32),
            pltpu.VMEM((CHUNKS, size, LANES), BF16),
            pltpu.VMEM((CHUNKS, size, LANES), BF16),
            pltpu.VMEM((CHUNKS, size, LANES), BF16),
            pltpu.VMEM((CHUNKS, size, LANES), BF16),
            pltpu.VMEM((CHUNKS, 2 * STEP, RROWS, LANES), BF16),
            pltpu.VMEM((CAP * EXP, TOK), BF16),
            pltpu.VMEM((CAP * EXP, FEAT), BF16),
            pltpu.VMEM((FEAT, HID), BF16),
            pltpu.VMEM((FEAT, HID), BF16),
            pltpu.VMEM((HID, FEAT), BF16),
            dma((2 * EXP,)),
            dma((CHUNKS,)),
            dma((CHUNKS,)),
            dma((CHUNKS,)),
            dma((CHUNKS,)),
            dma((CHUNKS,)),
            dma((2 * EXP,)),
            dma((CHUNKS,)),
            dma((3,)),
            dma((3,)),
        ],
        compiler_params=pltpu.CompilerParams(has_side_effects=True, vmem_limit_bytes=63_000_000),
    )(
        expert_ids.T,
        route_weights.astype(F32).T,
        tokens,
        out_grad,
        w_gate[0],
        w_up[0],
        w_down[0],
    )
    return (grad_tokens, grad_route.T.astype(BF16), grad_g[None], grad_u[None], grad_d[None])


def solution(mesh):
    rows_spec = P(("expert", "dp"), None)
    hidden_last = P("expert", None, "dp")
    hidden_mid = P("expert", "dp", None)
    return jax.shard_map(
        shards,
        mesh=mesh,
        in_specs=(rows_spec,) * 4 + (hidden_last, hidden_last, hidden_mid),
        out_specs=(rows_spec, rows_spec, hidden_last, hidden_last, hidden_mid),
        check_vma=False,
    )
```

time: 383 us -> 158 us (0.41)
  the two profiles are of different devices: /device:TPU:3 before, /device:TPU:8 now
where the time goes in v1:
time: 158 us
  Pallas kernels  147 us (93%)
  local copies, waits for them, and re-layouts  7.71 us (5%)
  other arithmetic  2.67 us (2%)
    pallas_call x1, Pallas kernels, shards(): pl.pallas_call(body, out_shape=(jax.ShapeDtypeStruct((TOK, FEAT), BF16),...  147 us
    unnamed x10, local copies, waits for them, and re-layouts  7.71 us

profile of v1, /device:TPU:8, one launch (start us, length us, event | category | flops | bytes accessed | tf_op | source)
XLA Modules:
  0.0 157.6 jit_solution(1489846933294168140)
XLA Ops:
  0.6 1.3 convert_bitcast_fusion.rw_ref
  1.9 146.5 %shard_map.110 = (bf16[128,3584]{1,0:T(8,128)(2,1)}, f32[8,128]{1,0:T(8,128)}, bf16[3584,256]{1,0:T(8,128)(2,1)}, bf16[3584,256]{1,0:T(8,128)(2,1)}, bf16[256,3584]{1,0:T(8,128)(2,1)}) custom-call(s32[8,128]{1,0:T(8,128)} %bitcast.17, f32[8,128]{1,0:T(8,128)} %convert_bitcast_fusion.rw_ref, bf16[128,3584]{1,0:T(8,128)(2,1)} %tok_ref.1, ...), custom_call_target="tpu_custom_call" | custom-call | tf_op jit(solution)/shard_map/pallas_call | solution.py:350
  148.4 0.0 copy-start.2
  148.5 1.4 convert_bitcast_fusion.1
  149.8 2.2 %copy.16 = bf16[128,3584]{1,0:T(8,128)(2,1)} copy(bf16[128,3584]{1,0:T(8,128)(2,1)} %get-tuple-element.20) | data formatting | bytes 1835008
  152.0 0.0 copy-done.2
  152.0 0.0 copy-start.1
  152.0 1.2 copy.17
  153.2 0.9 copy-done.1
  154.2 0.0 copy-start
  154.2 1.2 copy.18
  155.4 0.9 copy-done
  156.3 1.2 copy.19
Async XLA Ops:
  148.4 3.6 %copy-start.2 = (bf16[3584,256]{1,0:T(8,128)(2,1)S(1)}, bf16[3584,256]{1,0:T(8,128)(2,1)}, u32[]{:S(2)}) copy-start(bf16[3584,256]{1,0:T(8,128)(2,1)} %get-tuple-element.12) | copy-start | bytes 5505028
  152.0 2.2 %copy-start.1 = (bf16[3584,256]{1,0:T(8,128)(2,1)S(1)}, bf16[3584,256]{1,0:T(8,128)(2,1)}, u32[]{:S(2)}) copy-start(bf16[3584,256]{1,0:T(8,128)(2,1)} %get-tuple-element.13) | copy-start | bytes 5505028
  154.2 2.2 %copy-start = (bf16[256,3584]{1,0:T(8,128)(2,1)S(1)}, bf16[256,3584]{1,0:T(8,128)(2,1)}, u32[]{:S(2)}) copy-start(bf16[256,3584]{1,0:T(8,128)(2,1)} %get-tuple-element.14) | copy-start | bytes 5505028

commit v2 on v1

--- a/solution.py
+++ b/solution.py
@@ -24,25 +24,45 @@
 F32, BF16 = jnp.float32, jnp.bfloat16
 
 
+def steps(k):
+    kz = k & 3
+    return kz, (kz + (k >> 2)) & 3, (kz + (k >> 4)) & 1
+
+
 def shifted(e, k, sign):
     z, y, x = e // (NY * NX), (e // NX) % NY, e % NX
-    kz, ky, kx = k // (NY * NX), (k // NX) % NY, k % NX
-    z = (z + NZ + sign * kz) % NZ
-    y = (y + NY + sign * ky) % NY
-    x = (x + NX + sign * kx) % NX
+    kz, ky, kx = steps(k)
+    z = (z + NZ + sign * kz) & 3
+    y = (y + NY + sign * ky) & 3
+    x = (x + NX + sign * kx) & 1
     return (z * NY + y) * NX + x
 
 
 def body(
     ids_ref, rw_ref, tok_ref, dy_ref, wg_hbm, wu_hbm, wd_hbm,
-    gt_ref, gr_ref, gg_hbm, gu_hbm, gd_hbm,
-    wg, wu, wd, flat, send, recv, rows, dgu, wtd, retf, own, pst, prt, rsend, ret, slots, got, sg, su, sd,
-    send_sem, recv_sem, fws_sem, fwr_sem, pas_sem, par_sem, rs_sem, ret_sem, win_sem, out_sem,
+    gt_ref, gr_ref, sg, su, sd,
+    wg, wu, wd, flat, send, recv, rows, dgu, wtd, retf, own, pst, prt, rsend, ret, slots, early, got,
+    send_sem, recv_sem, fws_sem, fwr_sem, pas_sem, par_sem, rs_sem, ret_sem, win_sem,
 ):
     e = lax.axis_index("expert")
     d = lax.axis_index("dp")
     xl, c = d // 2, d % 2
     partner = {"expert": e, "dp": xl * 2 + 1 - c}
+
+    barrier = pltpu.get_barrier_semaphore()
+
+    def greet(k, xd):
+        there = {"expert": shifted(e, k, 1), "dp": xd * 2 + c}
+        pl.semaphore_signal(barrier, inc=1, device_id=there, device_id_type=MESH)
+
+    def greet_both(k, carry):
+        greet(k, 0)
+        greet(k, 1)
+        return carry
+
+    greet(0, 1 - xl)
+    pl.semaphore_signal(barrier, inc=1, device_id=partner, device_id_type=MESH)
+    lax.fori_loop(1, EXP, greet_both, 0)
 
     loads = [
         pltpu.make_async_copy(h, v, win_sem.at[i])
@@ -53,16 +73,16 @@
 
     kk = lax.broadcasted_iota(jnp.int32, (EXP, TOK), 0)
     z, y, x = e // (NY * NX), (e // NX) % NY, e % NX
-    tz = (z + (kk >> 3)) & 3
-    ty = (y + ((kk >> 1) & 3)) & 3
-    tx = (x + (kk & 1)) & 1
+    kz, ky, kx = steps(kk)
+    tz, ty, tx = (z + kz) & 3, (y + ky) & 3, (x + kx) & 1
     target = tz * (NY * NX) + ty * NX + tx
     chosen = jnp.zeros((EXP, TOK), F32)
     weight = jnp.zeros((EXP, TOK), F32)
+    rw = rw_ref[...].astype(F32)
     for q in range(8):
         same = ids_ref[q : q + 1, :] == target
         chosen = chosen + jnp.where(same, 1.0, 0.0)
-        weight = weight + jnp.where(same, rw_ref[q : q + 1, :], 0.0)
+        weight = weight + jnp.where(same, rw[q : q + 1, :], 0.0)
     before = lax.broadcasted_iota(jnp.int32, (TOK, TOK), 0) < lax.broadcasted_iota(
         jnp.int32, (TOK, TOK), 1
     )
@@ -72,27 +92,14 @@
     for j in range(CAP):
         hot = jnp.where(jnp.abs(rank - j) < 0.5, chosen, 0.0)
         slots[j * EXP : (j + 1) * EXP, :] = hot.astype(BF16)
+        for p in range(EXP // 8):
+            early[p, j * 8 : (j + 1) * 8, :] = hot[p * 8 : (p + 1) * 8, :]
         one = jnp.sum(hot * weight, axis=1, keepdims=True)
         flat[pl.ds(2 * CAP * COLS + j, EXP, stride=FROWS), :] = jnp.broadcast_to(one, (EXP, LANES))
     for j in range(2 * CAP * COLS + CAP, FROWS):
         flat[pl.ds(j, EXP, stride=FROWS), :] = jnp.zeros((EXP, LANES), F32)
     for j in range(CAP * COLS + 1, RROWS):
         retf[pl.ds(j, SRC, stride=RROWS), :] = jnp.zeros((SRC, LANES), F32)
-
-    def gather(m, carry):
-        for a, ref in enumerate((tok_ref, dy_ref)):
-            picked = jnp.dot(
-                slots[...], ref[:, pl.ds(pl.multiple_of(m * 256, 256), 256)], preferred_element_type=F32
-            )
-            for h in range(2):
-                for j in range(CAP):
-                    at = j * 2 * COLS + a * COLS + m * 2 + h
-                    flat[pl.ds(at, EXP, stride=FROWS), :] = picked[
-                        j * EXP : (j + 1) * EXP, h * LANES : (h + 1) * LANES
-                    ]
-        return carry
-
-    lax.fori_loop(0, FEAT // 256, gather, 0)
 
     def remote(k, xd):
         g, kq = k // STEP, k % STEP
@@ -105,17 +112,46 @@
             device_id_type=MESH,
         )
 
-    send[0] = flat[0:FROWS, :].astype(BF16)
+    def pack(k):
+        send[k] = flat[pl.ds(pl.multiple_of(k * FROWS, 8), FROWS), :].astype(BF16)
+
+    def issue(k, carry):
+        pack(k)
+        remote(k, 0).start()
+        remote(k, 1).start()
+        return carry
+
+    def pick(p):
+        hots = early[p].astype(BF16)
+
+        def gather(m, carry):
+            for a, ref in enumerate((tok_ref, dy_ref)):
+                picked = jnp.dot(
+                    hots, ref[:, pl.ds(pl.multiple_of(m * 256, 256), 256)], preferred_element_type=F32
+                )
+                for h in range(2):
+                    for j in range(CAP):
+                        at = p * 8 * FROWS + j * 2 * COLS + a * COLS + m * 2 + h
+                        flat[pl.ds(at, 8, stride=FROWS), :] = picked[
+                            j * 8 : (j + 1) * 8, h * LANES : (h + 1) * LANES
+                        ]
+            return carry
+
+        lax.fori_loop(0, FEAT // 256, gather, 0)
+
+    pick(0)
+    pack(0)
+    pl.semaphore_wait(barrier, 2 * EXP)
     remote(0, 1 - xl).start()
     pltpu.make_async_copy(send.at[0], recv.at[0, c * (2 * STEP) + xl], recv_sem.at[0]).start()
-
-    def issue(k, carry):
-        send[k] = flat[pl.ds(pl.multiple_of(k * FROWS, 8), FROWS), :].astype(BF16)
-        remote(k, 0).start()
-        remote(k, 1).start()
-        return carry
-
-    lax.fori_loop(1, EXP, issue, 0)
+    lax.fori_loop(1, 8, issue, 0)
+
+    def later(p, carry):
+        pick(p)
+        lax.fori_loop(p * 8, p * 8 + 8, issue, 0)
+        return carry
+
+    lax.fori_loop(1, EXP // 8, later, 0)
     for copy in loads:
         copy.wait()
 
@@ -266,13 +302,6 @@
         return carry
 
     lax.fori_loop(0, FEAT // 256, grads, 0)
-    stores = [
-        pltpu.make_async_copy(v, h, out_sem.at[i])
-        for i, (h, v) in enumerate(((gg_hbm, sg), (gu_hbm, su), (gd_hbm, sd)))
-    ]
-    for copy in stores:
-        copy.start()
-
     def collect(g, carry):
         pltpu.make_async_copy(ret.at[g], ret.at[g], ret_sem.at[g]).wait()
         for xs in range(2):
@@ -305,7 +334,7 @@
     for q in range(8):
         gr_ref[q : q + 1, :] = jnp.sum(
             jnp.where(ids_ref[q : q + 1, :] == target, spot, 0.0), axis=0, keepdims=True
-        )
+        ).astype(BF16)
 
     def place(m, carry):
         at = pl.ds(pl.multiple_of(m * 512, 512), 512)
@@ -314,8 +343,6 @@
 
     lax.fori_loop(0, FEAT // 512, place, 0)
 
-    for copy in stores:
-        copy.wait()
     remote(0, 1 - xl).wait_send()
     back(0, 0, 1 - xl).wait_send()
 
@@ -347,17 +374,12 @@
     anywhere = pl.BlockSpec(memory_space=pl.ANY)
     size = 2 * STEP * RROWS
     dma = pltpu.SemaphoreType.DMA
-    grad_tokens, grad_route, grad_g, grad_u, grad_d = pl.pallas_call(
+    shapes = ((TOK, FEAT), (8, TOK), (FEAT, HID), (FEAT, HID), (HID, FEAT))
+    made = pl.pallas_call(
         body,
-        out_shape=(
-            jax.ShapeDtypeStruct((TOK, FEAT), BF16),
-            jax.ShapeDtypeStruct((8, TOK), F32),
-            jax.ShapeDtypeStruct((FEAT, HID), BF16),
-            jax.ShapeDtypeStruct((FEAT, HID), BF16),
-            jax.ShapeDtypeStruct((HID, FEAT), BF16),
-        ),
+        out_shape=tuple(pltpu.VMEM(s, BF16) for s in shapes),
         in_specs=[vmem, vmem, vmem, vmem, anywhere, anywhere, anywhere],
-        out_specs=(vmem, vmem, anywhere, anywhere, anywhere),
+        out_specs=(vmem,) * 5,
         scratch_shapes=[
             pltpu.VMEM((FEAT, HID), BF16),
             pltpu.VMEM((FEAT, HID), BF16),
@@ -375,10 +397,8 @@
             pltpu.VMEM((CHUNKS, size, LANES), BF16),
             pltpu.VMEM((CHUNKS, 2 * STEP, RROWS, LANES), BF16),
             pltpu.VMEM((CAP * EXP, TOK), BF16),
+            pltpu.VMEM((EXP // 8, CAP * 8, TOK), F32),
             pltpu.VMEM((CAP * EXP, FEAT), BF16),
-            pltpu.VMEM((FEAT, HID), BF16),
-            pltpu.VMEM((FEAT, HID), BF16),
-            pltpu.VMEM((HID, FEAT), BF16),
             dma((2 * EXP,)),
             dma((CHUNKS,)),
             dma((CHUNKS,)),
@@ -387,20 +407,22 @@
             dma((CHUNKS,)),
             dma((2 * EXP,)),
             dma((CHUNKS,)),
-            dma((3,)),
             dma((3,)),
         ],
-        compiler_params=pltpu.CompilerParams(has_side_effects=True, vmem_limit_bytes=63_000_000),
+        compiler_params=pltpu.CompilerParams(
+            collective_id=0, has_side_effects=True, vmem_limit_bytes=50_000_000
+        ),
     )(
         expert_ids.T,
-        route_weights.astype(F32).T,
+        route_weights.T,
         tokens,
         out_grad,
         w_gate[0],
         w_up[0],
         w_down[0],
     )
-    return (grad_tokens, grad_route.T.astype(BF16), grad_g[None], grad_u[None], grad_d[None])
+    grad_tokens, grad_route, grad_g, grad_u, grad_d = made
+    return (grad_tokens, grad_route.T, grad_g[None], grad_u[None], grad_d[None])
 
 
 def solution(mesh):

time: 158 us -> 119 us (0.75)
  the two profiles are of different devices: /device:TPU:8 before, /device:TPU:3 now
where the time goes in v2:
time: 119 us; the launch traced here: 117 us
  Pallas kernels  110 us (92%)
  local copies, waits for them, and re-layouts  6.55 us (6%)
    pallas_call x1, Pallas kernels, shards(): pl.pallas_call(body, out_shape=tuple((pltpu.VMEM(s, BF16) for s in shapes...  110 us
    unnamed x9, local copies, waits for them, and re-layouts  6.55 us

profile of v2, /device:TPU:3, one launch (start us, length us, event | category | flops | bytes accessed | tf_op | source)
XLA Modules:
  0.0 117.1 jit_solution(12543416732781626076)
XLA Ops:
  0.6 0.0 copy-start
  0.6 0.7 copy-done
  1.3 0.0 copy-start.1
  1.3 0.7 copy-done.1
  2.0 109.9 %shard_map.110 = (bf16[128,3584]{1,0:T(8,128)(2,1)S(1)}, bf16[8,128]{1,0:T(8,128)(2,1)S(1)}, bf16[3584,256]{1,0:T(8,128)(2,1)S(1)}, bf16[3584,256]{1,0:T(8,128)(2,1)S(1)}, bf16[256,3584]{1,0:T(8,128)(2,1)S(1)}) custom-call(s32[8,128]{1,0:T(8,128)S(1)} %bitcast.13, bf16[8,128]{1,0:T(8,128)(2,1)S(1)} %bitcast.14, bf16[128,3584]{1,0:T(8,128)(2,1)} %tok_ref.1, ...), custom_call_target="tpu_custom_call" | custom-call | tf_op jit(solution)/shard_map/pallas_call | solution.py:378
  111.9 0.9 copy.17
  112.8 0.6 copy.18
  113.4 1.2 %copy.19 = bf16[1,3584,256]{2,1,0:T(8,128)(2,1)} copy(bf16[1,3584,256]{2,1,0:T(8,128)(2,1)S(1)} %bitcast.11) | data formatting | bytes 3670016
  114.6 1.2 %copy.20 = bf16[1,3584,256]{2,1,0:T(8,128)(2,1)} copy(bf16[1,3584,256]{2,1,0:T(8,128)(2,1)S(1)} %bitcast.10) | data formatting | bytes 3670016
  115.8 1.2 %copy.21 = bf16[1,256,3584]{2,1,0:T(8,128)(2,1)} copy(bf16[1,256,3584]{2,1,0:T(8,128)(2,1)S(1)} %bitcast.9) | data formatting | bytes 3670016
Async XLA Ops:
  0.6 0.7 copy-start
  1.3 0.7 copy-start.1

commit v3 on v2

v3 whole, which is shorter than its diff:
```python
import jax
import jax.numpy as jnp
from jax import lax
from jax.experimental import pallas as pl
from jax.experimental.pallas import tpu as pltpu
from jax.sharding import PartitionSpec as P

NZ, NY, NX = 4, 4, 2
EXP = NZ * NY * NX
CAP = 5
STEP = 4
CHUNKS = EXP // STEP
LANES = 128
FEAT = 3584
HID = 256
COLS = FEAT // LANES
FROWS = 288
RROWS = 144
FPITCH, RPITCH = FROWS + 1, RROWS + 1
SRC = 4 * STEP
ROWS = SRC * CAP
ALL = ROWS * CHUNKS
SPAN = 3 * ROWS
TOK = 128
MESH = pl.DeviceIdType.MESH
F32, BF16 = jnp.float32, jnp.bfloat16


def steps(k):
    kz = k & 3
    return kz, (kz + (k >> 2)) & 3, (kz + (k >> 4)) & 1


def shifted(e, k, sign):
    z, y, x = e >> 3, (e >> 1) & 3, e & 1
    kz, ky, kx = steps(k)
    z = (z + NZ + sign * kz) & 3
    y = (y + NY + sign * ky) & 3
    x = (x + NX + sign * kx) & 1
    return (z << 3) + (y << 1) + x


def targets(e):
    z, y, x = e >> 3, (e >> 1) & 3, e & 1
    kz, ky, kx = steps(lax.broadcasted_iota(jnp.int32, (EXP, TOK), 0))
    return (((z + kz) & 3) << 3) + (((y + ky) & 3) << 1) + ((x + kx) & 1)


def body(
    ids_ref, rw_ref, tok_ref, dy_ref, wg_hbm, wu_hbm, wd_hbm,
    flat, slots, sg, su, sd,
    wgu, wgut, wd, send, recv, rows, dgu, wtd, retf, own, pst, prt, rsend, ret, early,
    send_sem, recv_sem, fws_sem, fwr_sem, pas_sem, par_sem, rs_sem, ret_sem, win_sem,
):
    e = lax.axis_index("expert")
    d = lax.axis_index("dp")
    xl, c = d >> 1, d & 1
    partner = {"expert": e, "dp": xl * 2 + 1 - c}

    barrier = pltpu.get_barrier_semaphore()

    def greet(k, xd):
        there = {"expert": shifted(e, k, 1), "dp": xd * 2 + c}
        pl.semaphore_signal(barrier, inc=1, device_id=there, device_id_type=MESH)

    def greet_both(k, carry):
        greet(k, 0)
        greet(k, 1)
        return carry

    greet(0, 1 - xl)
    pl.semaphore_signal(barrier, inc=1, device_id=partner, device_id_type=MESH)
    lax.fori_loop(1, EXP, greet_both, 0)

    loads = [
        pltpu.make_async_copy(h, v, win_sem.at[i])
        for i, (h, v) in enumerate(((wg_hbm, wgu.at[:, 0:HID]), (wu_hbm, wgu.at[:, HID : 2 * HID]), (wd_hbm, wd)))
    ]
    for copy in loads:
        copy.start()

    target = targets(e)
    chosen = jnp.zeros((EXP, TOK), F32)
    weight = jnp.zeros((EXP, TOK), F32)
    rw = rw_ref[...].astype(F32)
    for q in range(8):
        same = ids_ref[q : q + 1, :] == target
        chosen = chosen + jnp.where(same, 1.0, 0.0)
        weight = weight + jnp.where(same, rw[q : q + 1, :], 0.0)
    before = lax.broadcasted_iota(jnp.int32, (TOK, TOK), 0) < lax.broadcasted_iota(
        jnp.int32, (TOK, TOK), 1
    )
    rank = jnp.dot(
        chosen.astype(BF16), jnp.where(before, 1.0, 0.0).astype(BF16), preferred_element_type=F32
    )
    for j in range(CAP):
        hot = jnp.where(jnp.abs(rank - j) < 0.5, chosen, 0.0)
        slots[j * EXP : (j + 1) * EXP, :] = hot.astype(BF16)
        for p in range(EXP // 8):
            early[p, j * 8 : (j + 1) * 8, :] = hot[p * 8 : (p + 1) * 8, :]
        one = jnp.sum(hot * weight, axis=1, keepdims=True)
        flat[pl.ds(2 * CAP * COLS + j, EXP, stride=FPITCH), :] = jnp.broadcast_to(one, (EXP, LANES))
    for j in range(2 * CAP * COLS + CAP, FROWS):
        flat[pl.ds(j, EXP, stride=FPITCH), :] = jnp.zeros((EXP, LANES), F32)
    for j in range(CAP * COLS + 1, RROWS):
        retf[pl.ds(j, SRC, stride=RPITCH), :] = jnp.zeros((SRC, LANES), F32)

    def remote(k, xd):
        g, kq = k >> 2, k & 3
        return pltpu.make_async_remote_copy(
            src_ref=send.at[k],
            dst_ref=recv.at[g, c * (2 * STEP) + kq * 2 + xl],
            send_sem=send_sem.at[k * 2 + xd],
            recv_sem=recv_sem.at[g],
            device_id={"expert": shifted(e, k, 1), "dp": xd * 2 + c},
            device_id_type=MESH,
        )

    def pack(k):
        send[k] = flat[pl.ds(k * FPITCH, FROWS), :].astype(BF16)

    def issue(k, carry):
        pack(k)
        remote(k, 0).start()
        remote(k, 1).start()
        return carry

    def pick(p):
        hots = early[p].astype(BF16)

        def gather(m, carry):
            for a, ref in enumerate((tok_ref, dy_ref)):
                picked = jnp.dot(
                    hots, ref[:, pl.ds(pl.multiple_of(m * 512, 512), 512)], preferred_element_type=F32
                )
                for h in range(4):
                    for j in range(CAP):
                        at = p * 8 * FPITCH + j * 2 * COLS + a * COLS + m * 4 + h
                        flat[pl.ds(at, 8, stride=FPITCH), :] = picked[
                            j * 8 : (j + 1) * 8, h * LANES : (h + 1) * LANES
                        ]
            return carry

        lax.fori_loop(0, FEAT // 512, gather, 0)

    pick(0)
    pack(0)
    pl.semaphore_wait(barrier, 2 * EXP)
    remote(0, 1 - xl).start()
    pltpu.make_async_copy(send.at[0], recv.at[0, c * (2 * STEP) + xl], recv_sem.at[0]).start()
    lax.fori_loop(1, 8, issue, 0)

    def later(p, carry):
        pick(p)
        lax.fori_loop(p * 8, p * 8 + 8, issue, 0)
        return carry

    lax.fori_loop(1, EXP // 8, later, 0)
    for copy in loads:
        copy.wait()

    def turn(m, carry):
        at = pl.ds(pl.multiple_of(m * 512, 512), 512)
        wgut[:, at] = wgu[at, :].T
        return carry

    lax.fori_loop(0, FEAT // 512, turn, 0)

    def half(g, core):
        return recv.at[g, pl.ds(core * (2 * STEP), 2 * STEP)]

    def forward(g):
        return pltpu.make_async_remote_copy(
            src_ref=half(g, c), dst_ref=half(g, c), send_sem=fws_sem.at[g], recv_sem=fwr_sem.at[g],
            device_id=partner, device_id_type=MESH,
        )

    def take(g):
        pltpu.make_async_copy(half(g, c), half(g, c), recv_sem.at[g]).wait()
        forward(g).start()

    def part(g):
        return pltpu.make_async_remote_copy(
            src_ref=pst.at[g], dst_ref=prt.at[g], send_sem=pas_sem.at[g], recv_sem=par_sem.at[g],
            device_id=partner, device_id_type=MESH,
        )

    def back(g, i, xs):
        kq = i // 2
        return pltpu.make_async_remote_copy(
            src_ref=rsend.at[g, pl.ds(pl.multiple_of((kq * 2 + xs) * RROWS, 16), RROWS)],
            dst_ref=ret.at[g, xl * STEP + kq],
            send_sem=rs_sem.at[g * (2 * STEP) + i],
            recv_sem=ret_sem.at[g],
            device_id={"expert": shifted(e, g * STEP + kq, -1), "dp": xs * 2 + c},
            device_id_type=MESH,
        )

    def compute(g):
        def widen(s, carry):
            flat[pl.ds(s * FPITCH, FROWS), :] = recv[g, s].astype(F32)
            return carry

        lax.fori_loop(0, SRC, widen, 0)
        base = pl.multiple_of(g * ROWS, 16)

        def order(q, carry):
            for h in range(4):
                col = q * 4 + h
                for j in range(CAP):
                    piece = flat[pl.ds(j * 2 * COLS + col, SRC, stride=FPITCH), :]
                    rows[
                        pl.ds(pl.multiple_of(base + j * SRC, 16), SRC),
                        pl.ds(pl.multiple_of(col * LANES, LANES), LANES),
                    ] = piece.astype(BF16)
            return carry

        lax.fori_loop(0, 2 * COLS // 4, order, 0)
        weights = jnp.concatenate(
            [flat[pl.ds(2 * CAP * COLS + j, SRC, stride=FPITCH), :] for j in range(CAP)], axis=0
        )
        weights = jnp.concatenate([weights, weights], axis=1)
        xs = rows[pl.ds(base, ROWS), 0:FEAT]
        dys = rows[pl.ds(base, ROWS), FEAT : 2 * FEAT]
        both = jnp.dot(xs, wgu[...], preferred_element_type=F32)
        gate, up = both[:, 0:HID], both[:, HID : 2 * HID]
        proj = lax.dot_general(dys, wd[...], (((1,), (1,)), ((), ())), preferred_element_type=F32)
        sig = jax.nn.sigmoid(gate)
        hidden = (gate * sig * up).astype(BF16).astype(F32)
        route = jnp.sum(hidden * proj, axis=1, keepdims=True)
        scaled = weights * proj
        d_gate = (scaled * up * sig * (1.0 + gate * (1.0 - sig))).astype(BF16)
        d_up = (scaled * gate * sig).astype(BF16)
        dgu[pl.ds(base, ROWS), 0:HID] = d_gate
        dgu[pl.ds(base, ROWS), HID : 2 * HID] = d_up
        wtd[pl.ds(base, ROWS), :] = (weights * hidden).astype(BF16)
        lane = lax.broadcasted_iota(jnp.int32, (SRC, LANES), 1)
        line = jnp.zeros((SRC, LANES), F32)
        for j in range(CAP):
            line = line + jnp.where(lane == j, route[j * SRC : (j + 1) * SRC, :], 0.0)
        retf[pl.ds(CAP * COLS, SRC, stride=RPITCH), :] = line

        def spread(m, carry):
            cols = pl.ds(pl.multiple_of(m * 512, 512), 512)
            piece = jnp.dot(dgu[pl.ds(base, ROWS), :], wgut[:, cols], preferred_element_type=F32)
            for h in range(4):
                for j in range(CAP):
                    retf[pl.ds(j * COLS + m * 4 + h, SRC, stride=RPITCH), :] = piece[
                        j * SRC : (j + 1) * SRC, h * LANES : (h + 1) * LANES
                    ]
            return carry

        lax.fori_loop(0, FEAT // 512, spread, 0)
        for ref, core in ((pst, 1 - c), (own, c)):
            for i in range(2 * STEP):
                ref[g, i * RROWS : (i + 1) * RROWS, :] = retf[
                    pl.ds((core * (2 * STEP) + i) * RPITCH, RROWS), :
                ].astype(BF16)
            if ref is pst:
                part(g).start()

    def reply(g):
        part(g).wait_recv()
        rsend[g] = (own[g].astype(F32) + prt[g].astype(F32)).astype(BF16)

    def local(g):
        return pltpu.make_async_copy(
            rsend.at[0, pl.ds(pl.multiple_of(xl * RROWS, 16), RROWS)], ret.at[0, xl * STEP], ret_sem.at[0]
        )

    def grads(low, high, first, last):
        tn = (((0,), (0,)), ((), ()))

        def tile(m, carry):
            at = pl.ds(pl.multiple_of(m * 512, 512), 512)
            far = pl.ds(pl.multiple_of(FEAT + m * 512, 512), 512)
            both = lax.dot_general(rows[low:high, at], dgu[low:high, :], tn, preferred_element_type=F32)
            down = lax.dot_general(wtd[low:high, :], rows[low:high, far], tn, preferred_element_type=F32)
            gate, up = both[:, 0:HID], both[:, HID : 2 * HID]
            if low > 0:
                gate, up = gate + sg[at, :].astype(F32), up + su[at, :].astype(F32)
                down = down + sd[:, at].astype(F32)
            sg[at, :] = gate.astype(BF16)
            su[at, :] = up.astype(BF16)
            sd[:, at] = down.astype(BF16)
            return carry

        lax.fori_loop(first, last, tile, 0)

    def chunk(g, carry):
        take(g)

        @pl.when(g == 1)
        def _():
            reply(0)
            local(0).start()
            back(0, 0, 1 - xl).start()
            for i in range(2, 2 * STEP):
                back(0, i, i % 2).start()

        @pl.when(g > 1)
        def _():
            reply(g - 1)
            for i in range(2 * STEP):
                back(g - 1, i, i % 2).start()

        @pl.when(g >= 4)
        def _():
            grads(0, SPAN, (g - 4) * 2, jnp.minimum((g - 4) * 2 + 2, FEAT // 512))

        forward(g).wait_recv()
        compute(g)
        return carry

    lax.fori_loop(0, CHUNKS, chunk, 0)
    reply(CHUNKS - 1)
    for i in range(2 * STEP):
        back(CHUNKS - 1, i, i % 2).start()

    grads(SPAN, ALL, 0, FEAT // 512)

    def collect(g, carry):
        pltpu.make_async_copy(ret.at[g], ret.at[g], ret_sem.at[g]).wait()
        for xs in range(2):
            for kq in range(STEP):
                at = (xs * EXP + g * STEP + kq) * RPITCH
                flat[pl.ds(at, RROWS), :] = ret[g, xs * STEP + kq].astype(F32)
        return carry

    lax.fori_loop(0, CHUNKS, collect, 0)

    remote(0, 1 - xl).wait_send()
    back(0, 0, 1 - xl).wait_send()

    def drain(k, carry):
        remote(k, 0).wait_send()
        remote(k, 1).wait_send()
        return carry

    lax.fori_loop(1, EXP, drain, 0)

    def drain_back(i, carry):
        pltpu.make_async_copy(
            rsend.at[0, pl.ds(0, RROWS)], rsend.at[0, pl.ds(0, RROWS)], rs_sem.at[i]
        ).wait()
        return carry

    lax.fori_loop(2, CHUNKS * 2 * STEP, drain_back, 0)

    def drain_pairs(g, carry):
        forward(g).wait_send()
        part(g).wait_send()
        return carry

    lax.fori_loop(0, CHUNKS, drain_pairs, 0)


def finish(
    ids_ref, flat, slots, sg, su, sd, gt_hbm, gr_hbm, gg_hbm, gu_hbm, gd_hbm, got, gtv, grv, sem
):
    pairs = ((sg, gg_hbm), (su, gu_hbm), (sd, gd_hbm), (gtv, gt_hbm), (grv, gr_hbm))
    copies = [pltpu.make_async_copy(v, h, sem.at[i]) for i, (v, h) in enumerate(pairs)]
    for copy in copies[:3]:
        copy.start()
    target = targets(lax.axis_index("expert"))
    tn = (((0,), (0,)), ((), ()))

    def merge(q, carry):
        for h in range(2):
            col = q * 2 + h
            for j in range(CAP):
                near = flat[pl.ds(j * COLS + col, EXP, stride=RPITCH), :]
                far = flat[pl.ds(EXP * RPITCH + j * COLS + col, EXP, stride=RPITCH), :]
                got[j * EXP : (j + 1) * EXP, pl.ds(pl.multiple_of(col * LANES, LANES), LANES)] = (
                    near + far
                ).astype(BF16)
        return carry

    lax.fori_loop(0, COLS // 2, merge, 0)
    line = (
        flat[pl.ds(CAP * COLS, EXP, stride=RPITCH), :]
        + flat[pl.ds(EXP * RPITCH + CAP * COLS, EXP, stride=RPITCH), :]
    )
    spot = jnp.zeros((EXP, TOK), F32)
    for j in range(CAP):
        spot = spot + slots[j * EXP : (j + 1) * EXP, :].astype(F32) * line[:, j : j + 1]
    for q in range(8):
        grv[q : q + 1, :] = jnp.sum(
            jnp.where(ids_ref[q : q + 1, :] == target, spot, 0.0), axis=0, keepdims=True
        ).astype(BF16)

    def place(m, carry):
        at = pl.ds(pl.multiple_of(m * 512, 512), 512)
        gtv[:, at] = lax.dot_general(slots[...], got[:, at], tn, preferred_element_type=F32).astype(BF16)
        return carry

    lax.fori_loop(0, FEAT // 512, place, 0)
    for copy in copies[3:]:
        copy.start()
    for copy in copies:
        copy.wait()


def shards(tokens, out_grad, expert_ids, route_weights, w_gate, w_up, w_down):
    vmem = pl.BlockSpec(memory_space=pltpu.VMEM)
    anywhere = pl.BlockSpec(memory_space=pl.ANY)
    size = 2 * STEP * RROWS
    dma = pltpu.SemaphoreType.DMA
    shapes = ((TOK, FEAT), (8, TOK), (FEAT, HID), (FEAT, HID), (HID, FEAT))
    kept = (((2 * EXP * RPITCH, LANES), F32), ((CAP * EXP, TOK), BF16)) + tuple((s, BF16) for s in shapes[2:])
    made = pl.pallas_call(
        body,
        out_shape=tuple(pltpu.VMEM(s, t) for s, t in kept),
        in_specs=[vmem, vmem, vmem, vmem, anywhere, anywhere, anywhere],
        out_specs=(vmem,) * 5,
        scratch_shapes=[
            pltpu.VMEM((FEAT, 2 * HID), BF16),
            pltpu.VMEM((2 * HID, FEAT), BF16),
            pltpu.VMEM((HID, FEAT), BF16),
            pltpu.VMEM((EXP, FROWS, LANES), BF16),
            pltpu.VMEM((CHUNKS, SRC, FROWS, LANES), BF16),
            pltpu.VMEM((ALL, 2 * FEAT), BF16),
            pltpu.VMEM((ALL, 2 * HID), BF16),
            pltpu.VMEM((ALL, HID), BF16),
            pltpu.VMEM((SRC * RPITCH, LANES), F32),
            pltpu.VMEM((CHUNKS, size, LANES), BF16),
            pltpu.VMEM((CHUNKS, size, LANES), BF16),
            pltpu.VMEM((CHUNKS, size, LANES), BF16),
            pltpu.VMEM((CHUNKS, size, LANES), BF16),
            pltpu.VMEM((CHUNKS, 2 * STEP, RROWS, LANES), BF16),
            pltpu.VMEM((EXP // 8, CAP * 8, TOK), F32),
            dma((2 * EXP,)),
            dma((CHUNKS,)),
            dma((CHUNKS,)),
            dma((CHUNKS,)),
            dma((CHUNKS,)),
            dma((CHUNKS,)),
            dma((2 * EXP,)),
            dma((CHUNKS,)),
            dma((3,)),
        ],
        compiler_params=pltpu.CompilerParams(
            collective_id=0, has_side_effects=True, vmem_limit_bytes=52_000_000
        ),
    )(
        expert_ids.T,
        route_weights.T,
        tokens,
        out_grad,
        w_gate[0],
        w_up[0],
        w_down[0],
    )
    made = [pltpu.with_memory_space_constraint(m, pltpu.VMEM) for m in made]
    grad_tokens, grad_route, grad_g, grad_u, grad_d = pl.pallas_call(
        finish,
        out_shape=tuple(jax.ShapeDtypeStruct(s, BF16) for s in shapes),
        in_specs=[vmem] * 6,
        out_specs=(anywhere,) * 5,
        scratch_shapes=[
            pltpu.VMEM((CAP * EXP, FEAT), BF16),
            pltpu.VMEM((TOK, FEAT), BF16),
            pltpu.VMEM((8, TOK), BF16),
            dma((5,)),
        ],
        compiler_params=pltpu.CompilerParams(vmem_limit_bytes=16_000_000),
    )(expert_ids.T, *made)
    return (grad_tokens, grad_route.T, grad_g[None], grad_u[None], grad_d[None])


def solution(mesh):
    rows_spec = P(("expert", "dp"), None)
    hidden_last = P("expert", None, "dp")
    hidden_mid = P("expert", "dp", None)
    return jax.shard_map(
        shards,
        mesh=mesh,
        in_specs=(rows_spec,) * 4 + (hidden_last, hidden_last, hidden_mid),
        out_specs=(rows_spec, rows_spec, hidden_last, hidden_last, hidden_mid),
        check_vma=False,
    )
```

time: 119 us -> 102 us (0.86); the launches traced: 117 us -> 101 us
  Pallas kernels: 110 us -> 101 us
  local copies, waits for them, and re-layouts: 6.55 us -> 0.01 us
    pallas_call x1 -> x2, Pallas kernels: 110 us -> 101 us  [the longest x1 97.8 us: shards(): pl.pallas_call(body, out_shape=tuple((pltpu.VMEM(s, t) for s, t in kept))...]
    unnamed x9 -> x2, local copies, waits for them, and re-layouts: 6.55 us -> 0.01 us
where the time goes in v3:
time: 102 us; the launch traced here: 101 us
  Pallas kernels  101 us (99%)
    pallas_call x1, Pallas kernels, shards(): pl.pallas_call(body, out_shape=tuple((pltpu.VMEM(s, t) for s, t in kept))...  97.8 us
    pallas_call x1, Pallas kernels, shards(): pl.pallas_call(finish, out_shape=tuple((jax.ShapeDtypeStruct(s, BF16) for...  2.94 us

profile of v3, /device:TPU:3, one launch (start us, length us, event | category | flops | bytes accessed | tf_op | source)
XLA Modules:
  0.0 101.4 jit_solution(13012048386331670644)
XLA Ops:
  0.6 0.0 copy-start
  0.6 97.8 %shard_map.110 = (f32[9280,128]{1,0:T(8,128)S(1)}, bf16[160,128]{1,0:T(8,128)(2,1)S(1)}, bf16[3584,256]{1,0:T(8,128)(2,1)S(1)}, bf16[3584,256]{1,0:T(8,128)(2,1)S(1)}, bf16[256,3584]{1,0:T(8,128)(2,1)S(1)}) custom-call(s32[8,128]{1,0:T(8,128)} %bitcast.9, bf16[8,128]{1,0:T(8,128)(2,1)} %bitcast.14, bf16[128,3584]{1,0:T(8,128)(2,1)} %tok_ref.1, ...), custom_call_target="tpu_custom_call" | custom-call | tf_op jit(solution)/shard_map/pallas_call | solution.py:411
  98.5 0.0 copy-done
  98.5 2.9 %shard_map.111 = (bf16[128,3584]{1,0:T(8,128)(2,1)}, bf16[8,128]{1,0:T(8,128)(2,1)}, bf16[3584,256]{1,0:T(8,128)(2,1)}, bf16[3584,256]{1,0:T(8,128)(2,1)}, bf16[256,3584]{1,0:T(8,128)(2,1)}) custom-call(s32[8,128]{1,0:T(8,128)S(1)} %bitcast.10, f32[9280,128]{1,0:T(8,128)S(1)} %get-tuple-element.15.flat, bf16[160,128]{1,0:T(8,128)(2,1)S(1)} %get-tuple-element.16.slots, ...), custom_call_target="tpu_custom_call" | custom-call | tf_op jit(solution)/shard_map/pallas_call | solution.py:455
Async XLA Ops:
  0.6 97.8 %copy-start = (s32[128,8]{0,1:T(8,128)S(1)}, s32[128,8]{0,1:T(8,128)}, u32[]{:S(2)}) copy-start(s32[128,8]{0,1:T(8,128)} %param.9) | copy-start | bytes 12292

commit v4 on v3

--- a/solution.py
+++ b/solution.py
@@ -20,7 +20,6 @@
 SRC = 4 * STEP
 ROWS = SRC * CAP
 ALL = ROWS * CHUNKS
-SPAN = 3 * ROWS
 TOK = 128
 MESH = pl.DeviceIdType.MESH
 F32, BF16 = jnp.float32, jnp.bfloat16
@@ -47,15 +46,22 @@
 
 
 def body(
-    ids_ref, rw_ref, tok_ref, dy_ref, wg_hbm, wu_hbm, wd_hbm,
+    ids_ref, rw_ref, tok_hbm, dy_hbm, wg_hbm, wu_hbm, wd_hbm,
     flat, slots, sg, su, sd,
-    wgu, wgut, wd, send, recv, rows, dgu, wtd, retf, own, pst, prt, rsend, ret, early,
-    send_sem, recv_sem, fws_sem, fwr_sem, pas_sem, par_sem, rs_sem, ret_sem, win_sem,
+    wgu, wgut, wd, send, recv, rows, dgu, wtd, retf, own, pst, prt, rsend, ret, early, tok_ref, dy_ref,
+    send_sem, recv_sem, fws_sem, fwr_sem, pas_sem, par_sem, rs_sem, ret_sem, win_sem, row_sem,
 ):
     e = lax.axis_index("expert")
     d = lax.axis_index("dp")
     xl, c = d >> 1, d & 1
     partner = {"expert": e, "dp": xl * 2 + 1 - c}
+
+    fetch = [
+        pltpu.make_async_copy(h, v, row_sem.at[i])
+        for i, (h, v) in enumerate(((tok_hbm, tok_ref), (dy_hbm, dy_ref)))
+    ]
+    for copy in fetch:
+        copy.start()
 
     barrier = pltpu.get_barrier_semaphore()
 
@@ -143,6 +149,8 @@
 
         lax.fori_loop(0, FEAT // 512, gather, 0)
 
+    for copy in fetch:
+        copy.wait()
     pick(0)
     pack(0)
     pl.semaphore_wait(barrier, 2 * EXP)
@@ -268,24 +276,21 @@
             rsend.at[0, pl.ds(pl.multiple_of(xl * RROWS, 16), RROWS)], ret.at[0, xl * STEP], ret_sem.at[0]
         )
 
-    def grads(low, high, first, last):
+    def grads():
         tn = (((0,), (0,)), ((), ()))
 
         def tile(m, carry):
             at = pl.ds(pl.multiple_of(m * 512, 512), 512)
             far = pl.ds(pl.multiple_of(FEAT + m * 512, 512), 512)
-            both = lax.dot_general(rows[low:high, at], dgu[low:high, :], tn, preferred_element_type=F32)
-            down = lax.dot_general(wtd[low:high, :], rows[low:high, far], tn, preferred_element_type=F32)
+            both = lax.dot_general(rows[:, at], dgu[:, :], tn, preferred_element_type=F32)
+            down = lax.dot_general(wtd[:, :], rows[:, far], tn, preferred_element_type=F32)
             gate, up = both[:, 0:HID], both[:, HID : 2 * HID]
-            if low > 0:
-                gate, up = gate + sg[at, :].astype(F32), up + su[at, :].astype(F32)
-                down = down + sd[:, at].astype(F32)
             sg[at, :] = gate.astype(BF16)
             su[at, :] = up.astype(BF16)
             sd[:, at] = down.astype(BF16)
             return carry
 
-        lax.fori_loop(first, last, tile, 0)
+        lax.fori_loop(0, FEAT // 512, tile, 0)
 
     def chunk(g, carry):
         take(g)
@@ -304,10 +309,6 @@
             for i in range(2 * STEP):
                 back(g - 1, i, i % 2).start()
 
-        @pl.when(g >= 4)
-        def _():
-            grads(0, SPAN, (g - 4) * 2, jnp.minimum((g - 4) * 2 + 2, FEAT // 512))
-
         forward(g).wait_recv()
         compute(g)
         return carry
@@ -317,7 +318,7 @@
     for i in range(2 * STEP):
         back(CHUNKS - 1, i, i % 2).start()
 
-    grads(SPAN, ALL, 0, FEAT // 512)
+    grads()
 
     def collect(g, carry):
         pltpu.make_async_copy(ret.at[g], ret.at[g], ret_sem.at[g]).wait()
@@ -411,7 +412,7 @@
     made = pl.pallas_call(
         body,
         out_shape=tuple(pltpu.VMEM(s, t) for s, t in kept),
-        in_specs=[vmem, vmem, vmem, vmem, anywhere, anywhere, anywhere],
+        in_specs=[vmem, vmem] + [anywhere] * 5,
         out_specs=(vmem,) * 5,
         scratch_shapes=[
             pltpu.VMEM((FEAT, 2 * HID), BF16),
@@ -429,6 +430,8 @@
             pltpu.VMEM((CHUNKS, size, LANES), BF16),
             pltpu.VMEM((CHUNKS, 2 * STEP, RROWS, LANES), BF16),
             pltpu.VMEM((EXP // 8, CAP * 8, TOK), F32),
+            pltpu.VMEM((TOK, FEAT), BF16),
+            pltpu.VMEM((TOK, FEAT), BF16),
             dma((2 * EXP,)),
             dma((CHUNKS,)),
             dma((CHUNKS,)),
@@ -438,6 +441,7 @@
             dma((2 * EXP,)),
             dma((CHUNKS,)),
             dma((3,)),
+            dma((2,)),
         ],
         compiler_params=pltpu.CompilerParams(
             collective_id=0, has_side_effects=True, vmem_limit_bytes=52_000_000

time: 102 us -> 100 us (0.980)
  Pallas kernels: 101 us -> 99.7 us
    pallas_call x1, Pallas kernels: 97.8 us -> 96.7 us  [shards(): pl.pallas_call(body, out_shape=tuple((pltpu.VMEM(s, t) for s, t in kept))...]
where the time goes in v4:
time: 100 us
  Pallas kernels  99.7 us (100%)
    pallas_call x1, Pallas kernels, shards(): pl.pallas_call(body, out_shape=tuple((pltpu.VMEM(s, t) for s, t in kept))...  96.7 us
    pallas_call x1, Pallas kernels, shards(): pl.pallas_call(finish, out_shape=tuple((jax.ShapeDtypeStruct(s, BF16) for...  2.94 us

profile of v4, /device:TPU:3, one launch (start us, length us, event | category | flops | bytes accessed | tf_op | source)
XLA Modules:
  0.0 100.3 jit_solution(16793694223838101479)
XLA Ops:
  0.6 0.0 copy-start
  0.6 96.7 %shard_map.110 = (f32[9280,128]{1,0:T(8,128)S(1)}, bf16[160,128]{1,0:T(8,128)(2,1)S(1)}, bf16[3584,256]{1,0:T(8,128)(2,1)S(1)}, bf16[3584,256]{1,0:T(8,128)(2,1)S(1)}, bf16[256,3584]{1,0:T(8,128)(2,1)S(1)}) custom-call(s32[8,128]{1,0:T(8,128)} %bitcast.9, bf16[8,128]{1,0:T(8,128)(2,1)} %bitcast.14, bf16[128,3584]{1,0:T(8,128)(2,1)} %tok_hbm.1, ...), custom_call_target="tpu_custom_call" | custom-call | tf_op jit(solution)/shard_map/pallas_call | solution.py:412
  97.4 0.0 copy-done
  97.4 2.9 %shard_map.111 = (bf16[128,3584]{1,0:T(8,128)(2,1)}, bf16[8,128]{1,0:T(8,128)(2,1)}, bf16[3584,256]{1,0:T(8,128)(2,1)}, bf16[3584,256]{1,0:T(8,128)(2,1)}, bf16[256,3584]{1,0:T(8,128)(2,1)}) custom-call(s32[8,128]{1,0:T(8,128)S(1)} %bitcast.10, f32[9280,128]{1,0:T(8,128)S(1)} %get-tuple-element.15.flat, bf16[160,128]{1,0:T(8,128)(2,1)S(1)} %get-tuple-element.16.slots, ...), custom_call_target="tpu_custom_call" | custom-call | tf_op jit(solution)/shard_map/pallas_call | solution.py:459
Async XLA Ops:
  0.6 96.8 %copy-start = (s32[128,8]{0,1:T(8,128)S(1)}, s32[128,8]{0,1:T(8,128)}, u32[]{:S(2)}) copy-start(s32[128,8]{0,1:T(8,128)} %param.9) | copy-start | bytes 12292

commit v5 on v4

--- a/solution.py
+++ b/solution.py
@@ -17,6 +17,7 @@
 FROWS = 288
 RROWS = 144
 FPITCH, RPITCH = FROWS + 1, RROWS + 1
+SPARE = 320
 SRC = 4 * STEP
 ROWS = SRC * CAP
 ALL = ROWS * CHUNKS
@@ -393,11 +394,11 @@
     def place(m, carry):
         at = pl.ds(pl.multiple_of(m * 512, 512), 512)
         gtv[:, at] = lax.dot_general(slots[...], got[:, at], tn, preferred_element_type=F32).astype(BF16)
-        return carry
-
+        pltpu.make_async_copy(gtv.at[:, at], gt_hbm.at[:, at], sem.at[3]).start()
+        return carry
+
+    copies[4].start()
     lax.fori_loop(0, FEAT // 512, place, 0)
-    for copy in copies[3:]:
-        copy.start()
     for copy in copies:
         copy.wait()
 
@@ -408,7 +409,7 @@
     size = 2 * STEP * RROWS
     dma = pltpu.SemaphoreType.DMA
     shapes = ((TOK, FEAT), (8, TOK), (FEAT, HID), (FEAT, HID), (HID, FEAT))
-    kept = (((2 * EXP * RPITCH, LANES), F32), ((CAP * EXP, TOK), BF16)) + tuple((s, BF16) for s in shapes[2:])
+    kept = (((2 * EXP * RPITCH + SPARE, LANES), F32), ((CAP * EXP, TOK), BF16)) + tuple((s, BF16) for s in shapes[2:])
     made = pl.pallas_call(
         body,
         out_shape=tuple(pltpu.VMEM(s, t) for s, t in kept),
@@ -423,7 +424,7 @@
             pltpu.VMEM((ALL, 2 * FEAT), BF16),
             pltpu.VMEM((ALL, 2 * HID), BF16),
             pltpu.VMEM((ALL, HID), BF16),
-            pltpu.VMEM((SRC * RPITCH, LANES), F32),
+            pltpu.VMEM((SRC * RPITCH + SPARE, LANES), F32),
             pltpu.VMEM((CHUNKS, size, LANES), BF16),
             pltpu.VMEM((CHUNKS, size, LANES), BF16),
             pltpu.VMEM((CHUNKS, size, LANES), BF16),

time: 100 us -> 100 us (level)
  no operation moved by 1% of the time
where the time goes in v5:
time: 100 us
  Pallas kernels  99.5 us (100%)
    pallas_call x1, Pallas kernels, shards(): pl.pallas_call(body, out_shape=tuple((pltpu.VMEM(s, t) for s, t in kept))...  96.7 us
    pallas_call x1, Pallas kernels, shards(): pl.pallas_call(finish, out_shape=tuple((jax.ShapeDtypeStruct(s, BF16) for...  2.75 us

profile of v5, /device:TPU:3, one launch (start us, length us, event | category | flops | bytes accessed | tf_op | source)
XLA Modules:
  0.0 100.1 jit_solution(416250966074347272)
XLA Ops:
  0.6 0.0 copy-start
  0.6 96.7 %shard_map.110 = (f32[9600,128]{1,0:T(8,128)S(1)}, bf16[160,128]{1,0:T(8,128)(2,1)S(1)}, bf16[3584,256]{1,0:T(8,128)(2,1)S(1)}, bf16[3584,256]{1,0:T(8,128)(2,1)S(1)}, bf16[256,3584]{1,0:T(8,128)(2,1)S(1)}) custom-call(s32[8,128]{1,0:T(8,128)} %bitcast.9, bf16[8,128]{1,0:T(8,128)(2,1)} %bitcast.14, bf16[128,3584]{1,0:T(8,128)(2,1)} %tok_hbm.1, ...), custom_call_target="tpu_custom_call" | custom-call | tf_op jit(solution)/shard_map/pallas_call | solution.py:413
  97.4 0.0 copy-done
  97.4 2.8 %shard_map.111 = (bf16[128,3584]{1,0:T(8,128)(2,1)}, bf16[8,128]{1,0:T(8,128)(2,1)}, bf16[3584,256]{1,0:T(8,128)(2,1)}, bf16[3584,256]{1,0:T(8,128)(2,1)}, bf16[256,3584]{1,0:T(8,128)(2,1)}) custom-call(s32[8,128]{1,0:T(8,128)S(1)} %bitcast.10, f32[9600,128]{1,0:T(8,128)S(1)} %get-tuple-element.15.flat, bf16[160,128]{1,0:T(8,128)(2,1)S(1)} %get-tuple-element.16.slots, ...), custom_call_target="tpu_custom_call" | custom-call | tf_op jit(solution)/shard_map/pallas_call | solution.py:460
Async XLA Ops:
  0.6 96.8 %copy-start = (s32[128,8]{0,1:T(8,128)S(1)}, s32[128,8]{0,1:T(8,128)}, u32[]{:S(2)}) copy-start(s32[128,8]{0,1:T(8,128)} %param.9) | copy-start | bytes 12292
